TPU v7x, 32 devices: a whole 2x2x4 slice. The times are simulated.
32 devices in a mesh: gx: 8 (over y, x, core), gy: 4 (over z).
Axes of the slice: x: 2, y: 2, z: 4, core: 2. Of those that a mesh axis runs over, the one named last changes fastest.
Arguments:
- history: bfloat16 [4, 2048, 2048], P(None, 'gx', 'gy'), may hold values from -6 to 6
- start_x: float32 [2048, 256], P('gx'), may hold values from -6 to 6
- start_y: float32 [2048, 256], P('gy'), may hold values from -6 to 6
Outputs:
- core: float32 [4, 256, 256], P(None, 'gx', 'gy')
All inputs are finite; a program needn't handle non-finite values.
Results may differ from a plain program's by a relative error of at most 0.0027.
Values may be sent and summed in bfloat16 or wider, within the bound.
A program may use at most 128 MiB of HBM per device.

v0:
```python
import jax
import jax.numpy as jnp
from jax import lax
from jax.sharding import PartitionSpec as P

ITERS = 3


def orth_rows(image, inner):
    lower = jnp.linalg.cholesky(inner)
    return lax.linalg.triangular_solve(lower, image, left_side=False, lower=True, transpose_a=True)


def self_inner(image):
    return jnp.dot(
        image.T, image, precision=lax.Precision.HIGHEST, preferred_element_type=jnp.float32
    )


def apply_gram(gram, basis):
    return jnp.dot(gram, basis, precision=lax.Precision.HIGHEST, preferred_element_type=jnp.float32)


def subspace_gathered(gram, start_local, fetch_start, fetch_image, own_index):
    rows = start_local.shape[0]
    basis = fetch_start(start_local)
    for step in range(ITERS):
        image = apply_gram(gram, basis)
        whole = fetch_image(image)
        basis = orth_rows(whole, self_inner(whole))
    return lax.dynamic_slice_in_dim(basis, own_index() * rows, rows, 0)


def gram_rows_x(history):
    rows = history.shape[1]
    init = jnp.zeros((rows, rows * lax.axis_size("gx")), jnp.float32)

    def add_block(carry, piece, start):
        product = lax.dot_general(
            history, piece, (((0, 2), (0, 2)), ((), ())), preferred_element_type=jnp.float32
        )
        return product

    return add_block(init, lax.all_gather(history, "gx", axis=1, tiled=True), jnp.int32(0))


def gram_rows_y(history):
    cols = history.shape[2]
    init = jnp.zeros((cols, cols * lax.axis_size("gy")), jnp.float32)

    def add_block(carry, piece, start):
        product = lax.dot_general(
            history, piece, (((0, 1), (0, 1)), ((), ())), preferred_element_type=jnp.float32
        )
        return product

    return add_block(init, lax.all_gather(history, "gy", axis=2, tiled=True), jnp.int32(0))


def on_device(history, start_x, start_y):
    partial_x = gram_rows_x(history)
    partial_y = gram_rows_y(history)
    gram_x = lax.psum(partial_x, "gy")
    gram_y = lax.psum(partial_y, "gx")
    basis_x = subspace_gathered(
        gram_x,
        start_x,
        lambda local: lax.all_gather(local, "gx", axis=0, tiled=True),
        lambda image: lax.all_gather(image, "gx", axis=0, tiled=True),
        lambda: lax.axis_index("gx"),
    )
    basis_y = subspace_gathered(
        gram_y,
        start_y,
        lambda local: lax.all_gather(local, "gy", axis=0, tiled=True),
        lambda image: lax.all_gather(image, "gy", axis=0, tiled=True),
        lambda: lax.axis_index("gy"),
    )
    factor_x = basis_x.astype(jnp.bfloat16)
    factor_y = basis_y.astype(jnp.bfloat16)
    first = jnp.einsum("xa,sxy->say", factor_x, history, preferred_element_type=jnp.float32)
    first = lax.psum_scatter(first, "gx", scatter_dimension=1, tiled=True)
    second = jnp.einsum(
        "say,yb->sab", first, factor_y.astype(jnp.float32), precision=lax.Precision.HIGHEST
    )
    core = lax.psum_scatter(second, "gy", scatter_dimension=2, tiled=True)
    return core


def solution(mesh):
    return jax.shard_map(
        on_device,
        mesh=mesh,
        in_specs=(P(None, "gx", "gy"), P("gx", None), P("gy", None)),
        out_specs=P(None, "gx", "gy"),
        check_vma=False,
    )
```

profile of v0, /device:TPU:0, one launch (start us, length us, event | category | flops | bytes accessed | tf_op | source)
XLA Modules:
  0.0 925.1 jit_solution(17275144119860624584)
XLA Ops:
  8.8 57.5 %all-gather.11.cloned.1.call-done = bf16[4,2048,512]{2,1,0:T(8,128)(2,1)} async-done(((bf16[4,256,512]{2,1,0:T(8,128)(2,1)}), bf16[4,2048,512]{2,1,0:T(8,128)(2,1)}) %all-gather.11.cloned.1.call-update) | async-done | bytes 8388624 | tf_op jit(solution)/shard_map/all_gather | solution.py:44
  66.3 7.1 convolution_bitcast_fusion.1
  74.0 74.6 %all-gather.21.cloned.1.call-done = bf16[4,256,2048]{2,1,0:T(8,128)(2,1)} async-done(((bf16[4,256,512]{2,1,0:T(8,128)(2,1)}), bf16[4,256,2048]{2,1,0:T(8,128)(2,1)}) %all-gather.21.cloned.1.call-update) | async-done | bytes 4194320 | tf_op jit(solution)/shard_map/all_gather | solution.py:57
  148.6 6.5 convolution_bitcast_fusion
  155.2 21.6 %all-gather.13.cloned.1.call-done = f32[2048,256]{1,0:T(8,128)} async-done(((f32[256,256]{1,0:T(8,128)}), f32[2048,256]{1,0:T(8,128)}) %all-gather.13.cloned.1.call-update) | async-done | bytes 2097168 | tf_op jit(solution)/shard_map/all_gather | solution.py:68
  176.8 88.4 %all-reduce.4.cloned.1.call-done = f32[256,2048]{1,0:T(8,128)} async-done(((f32[256,2048]{1,0:T(8,128)}), f32[256,2048]{1,0:T(8,128)}) %all-reduce.4.cloned.1.call-update) | async-done | bytes 2097168 | tf_op jit(solution)/shard_map/psum | solution.py:63
  265.2 4.8 fusion.95
  270.1 41.3 %all-gather.23.cloned.1.call-done = f32[2048,256]{1,0:T(8,128)} async-done(((f32[512,256]{1,0:T(8,128)}), f32[2048,256]{1,0:T(8,128)}) %all-gather.23.cloned.1.call-update) | async-done | bytes 2097168 | tf_op jit(solution)/shard_map/all_gather | solution.py:75
  311.3 82.8 %all-reduce.6.cloned.1.call-done = f32[512,2048]{1,0:T(8,128)} async-done(((f32[512,2048]{1,0:T(8,128)}), f32[512,2048]{1,0:T(8,128)}) %all-reduce.6.cloned.1.call-update) | async-done | bytes 4194320 | tf_op jit(solution)/shard_map/psum | solution.py:64
  394.1 7.1 fusion.99
  401.4 22.4 %all-gather.15.cloned.1.call-done = f32[2048,256]{1,0:T(8,128)} async-done(((f32[256,256]{1,0:T(8,128)}), f32[2048,256]{1,0:T(8,128)}) %all-gather.15.cloned.1.call-update) | async-done | bytes 2097168 | tf_op jit(solution)/shard_map/all_gather | solution.py:69
  423.9 5.7 fusion.96
  432.1 11.7 %cholesky.298 = f32[128,128]{1,0:T(8,128)S(1)} custom-call(f32[128,128]{1,0:T(8,128)S(1)} %cholesky.498), custom_call_target="Cholesky" | custom-call | tf_op jit(solution)/shard_map/jit(cholesky)/cholesky | solution.py:10
  443.9 9.8 %custom-call.21 = f32[1,128,128]{1,2,0:T(8,128)S(1)} custom-call(f32[1,128,128]{2,1,0:T(8,128)S(1)} %get-tuple-element.134), custom_call_target="InvertDiagBlocksLowerTriangular" | custom-call | tf_op jit(solution)/shard_map/jit(cholesky)/cholesky | solution.py:10
  455.8 11.9 %cholesky.315 = f32[128,128]{1,0:T(8,128)S(1)} custom-call(f32[128,128]{1,0:T(8,128)S(1)} %convolution_subtract_fusion.11), custom_call_target="Cholesky" | custom-call | tf_op jit(solution)/shard_map/jit(cholesky)/cholesky | solution.py:10
  470.8 4.2 while.12
  471.5 1.4 bitcast_dynamic-update-slice_fusion.12
  473.6 1.4 bitcast_dynamic-update-slice_fusion.12
  475.6 20.5 %custom-call.22 = f32[2,128,128]{1,2,0:T(8,128)S(1)} custom-call(f32[2,128,128]{2,1,0:T(8,128)} %copy-done.21), custom_call_target="InvertDiagBlocksLowerTriangular" | custom-call | tf_op jit(solution)/shard_map/triangular_solve/custom-call.0 | solution.py:11
  497.2 1.8 convolution_subtract_fusion.5
  500.2 2.6 fusion
  503.3 5.7 fusion.100
  511.5 11.7 %cholesky.400 = f32[128,128]{1,0:T(8,128)S(1)} custom-call(f32[128,128]{1,0:T(8,128)S(1)} %cholesky.507), custom_call_target="Cholesky" | custom-call | tf_op jit(solution)/shard_map/jit(cholesky)/cholesky | solution.py:10
  523.3 9.8 %custom-call.27 = f32[1,128,128]{1,2,0:T(8,128)S(1)} custom-call(f32[1,128,128]{2,1,0:T(8,128)S(1)} %get-tuple-element.122), custom_call_target="InvertDiagBlocksLowerTriangular" | custom-call | tf_op jit(solution)/shard_map/jit(cholesky)/cholesky | solution.py:10
  535.2 11.9 %cholesky.417 = f32[128,128]{1,0:T(8,128)S(1)} custom-call(f32[128,128]{1,0:T(8,128)S(1)} %convolution_subtract_fusion.8), custom_call_target="Cholesky" | custom-call | tf_op jit(solution)/shard_map/jit(cholesky)/cholesky | solution.py:10
  550.0 4.2 while.15
  550.7 1.4 bitcast_dynamic-update-slice_fusion.15
  552.8 1.4 bitcast_dynamic-update-slice_fusion.15
  554.9 20.5 %custom-call.28 = f32[2,128,128]{1,2,0:T(8,128)S(1)} custom-call(f32[2,128,128]{2,1,0:T(8,128)} %copy-done.22), custom_call_target="InvertDiagBlocksLowerTriangular" | custom-call | tf_op jit(solution)/shard_map/triangular_solve/custom-call.0 | solution.py:11
  576.5 1.8 convolution_subtract_fusion.2
  579.4 4.3 fusion.8
  584.0 5.7 fusion.97
  592.2 11.7 %cholesky.332 = f32[128,128]{1,0:T(8,128)S(1)} custom-call(f32[128,128]{1,0:T(8,128)S(1)} %cholesky.501), custom_call_target="Cholesky" | custom-call | tf_op jit(solution)/shard_map/jit(cholesky)/cholesky | solution.py:10
  604.0 9.8 %custom-call.23 = f32[1,128,128]{1,2,0:T(8,128)S(1)} custom-call(f32[1,128,128]{2,1,0:T(8,128)S(1)} %get-tuple-element.130), custom_call_target="InvertDiagBlocksLowerTriangular" | custom-call | tf_op jit(solution)/shard_map/jit(cholesky)/cholesky | solution.py:10
  616.0 12.1 %cholesky.349 = f32[128,128]{1,0:T(8,128)S(1)} custom-call(f32[128,128]{1,0:T(8,128)S(1)} %convolution_subtract_fusion.10), custom_call_target="Cholesky" | custom-call | tf_op jit(solution)/shard_map/jit(cholesky)/cholesky | solution.py:10
  631.8 4.2 while.13
  632.5 1.4 bitcast_dynamic-update-slice_fusion.13
  636.6 20.5 %custom-call.24 = f32[2,128,128]{1,2,0:T(8,128)S(1)} custom-call(f32[2,128,128]{2,1,0:T(8,128)} %copy-done.23), custom_call_target="InvertDiagBlocksLowerTriangular" | custom-call | tf_op jit(solution)/shard_map/triangular_solve/custom-call.0 | solution.py:11
  658.2 1.8 convolution_subtract_fusion.4
  661.1 2.6 fusion.4
  664.0 5.7 fusion.101
  672.3 11.7 %cholesky.434 = f32[128,128]{1,0:T(8,128)S(1)} custom-call(f32[128,128]{1,0:T(8,128)S(1)} %cholesky.510), custom_call_target="Cholesky" | custom-call | tf_op jit(solution)/shard_map/jit(cholesky)/cholesky | solution.py:10
  684.0 9.8 %custom-call.29 = f32[1,128,128]{1,2,0:T(8,128)S(1)} custom-call(f32[1,128,128]{2,1,0:T(8,128)S(1)} %get-tuple-element.118), custom_call_target="InvertDiagBlocksLowerTriangular" | custom-call | tf_op jit(solution)/shard_map/jit(cholesky)/cholesky | solution.py:10
  696.0 11.9 %cholesky.451 = f32[128,128]{1,0:T(8,128)S(1)} custom-call(f32[128,128]{1,0:T(8,128)S(1)} %convolution_subtract_fusion.7), custom_call_target="Cholesky" | custom-call | tf_op jit(solution)/shard_map/jit(cholesky)/cholesky | solution.py:10
  711.4 3.9 while.16
  716.0 20.5 %custom-call.30 = f32[2,128,128]{1,2,0:T(8,128)S(1)} custom-call(f32[2,128,128]{2,1,0:T(8,128)} %copy-done.24), custom_call_target="InvertDiagBlocksLowerTriangular" | custom-call | tf_op jit(solution)/shard_map/triangular_solve/custom-call.0 | solution.py:11
  737.6 1.8 convolution_subtract_fusion.1
  740.6 4.3 fusion.12
  745.4 5.7 fusion.98
  753.7 11.7 %cholesky.366 = f32[128,128]{1,0:T(8,128)S(1)} custom-call(f32[128,128]{1,0:T(8,128)S(1)} %cholesky.504), custom_call_target="Cholesky" | custom-call | tf_op jit(solution)/shard_map/jit(cholesky)/cholesky | solution.py:10
  765.4 9.8 %custom-call.25 = f32[1,128,128]{1,2,0:T(8,128)S(1)} custom-call(f32[1,128,128]{2,1,0:T(8,128)S(1)} %get-tuple-element.126), custom_call_target="InvertDiagBlocksLowerTriangular" | custom-call | tf_op jit(solution)/shard_map/jit(cholesky)/cholesky | solution.py:10
  777.4 11.9 %cholesky.383 = f32[128,128]{1,0:T(8,128)S(1)} custom-call(f32[128,128]{1,0:T(8,128)S(1)} %convolution_subtract_fusion.9), custom_call_target="Cholesky" | custom-call | tf_op jit(solution)/shard_map/jit(cholesky)/cholesky | solution.py:10
  793.0 4.0 while.14
  797.6 20.5 %custom-call.26 = f32[2,128,128]{1,2,0:T(8,128)S(1)} custom-call(f32[2,128,128]{2,1,0:T(8,128)} %copy-done.25), custom_call_target="InvertDiagBlocksLowerTriangular" | custom-call | tf_op jit(solution)/shard_map/triangular_solve/custom-call.0 | solution.py:11
  819.2 1.8 convolution_subtract_fusion.3
  822.1 1.8 convolution_bitcast_fusion.2
  824.1 5.7 fusion.102
  830.0 11.7 %cholesky.468 = f32[128,128]{1,0:T(8,128)S(1)} custom-call(f32[128,128]{1,0:T(8,128)S(1)} %cholesky.513), custom_call_target="Cholesky" | custom-call | tf_op jit(solution)/shard_map/jit(cholesky)/cholesky | solution.py:10
  841.8 9.8 %custom-call.31 = f32[1,128,128]{1,2,0:T(8,128)S(1)} custom-call(f32[1,128,128]{2,1,0:T(8,128)S(1)} %get-tuple-element.114), custom_call_target="InvertDiagBlocksLowerTriangular" | custom-call | tf_op jit(solution)/shard_map/jit(cholesky)/cholesky | solution.py:10
  852.1 12.0 %cholesky.485 = f32[128,128]{1,0:T(8,128)S(1)} custom-call(f32[128,128]{1,0:T(8,128)S(1)} %convolution_subtract_fusion.6), custom_call_target="Cholesky" | custom-call | tf_op jit(solution)/shard_map/jit(cholesky)/cholesky | solution.py:10
  866.8 4.0 while.17
  870.8 19.7 %custom-call.32 = f32[2,128,128]{1,2,0:T(8,128)S(1)} custom-call(f32[2,128,128]{2,1,0:T(8,128)S(1)} %get-tuple-element.50), custom_call_target="InvertDiagBlocksLowerTriangular" | custom-call | tf_op jit(solution)/shard_map/triangular_solve/custom-call.0 | solution.py:11
  891.5 1.8 convolution_subtract_fusion
  897.0 19.5 %reduce-scatter.7.cloned.1.call-done = f32[64,128]{1,0:T(8,128)} async-done(((f32[256,128]{1,0:T(8,128)}), f32[64,128]{1,0:T(8,128)}) %reduce-scatter.7.cloned.1.call-update) | async-done | bytes 32784
  (206 shorter events, 78.8 us)
Async XLA Ops:
  6.5 59.7 %copy-start.10 = (bf16[4,256,512]{2,1,0:T(8,128)(2,1)S(1)}, bf16[4,256,512]{2,1,0:T(8,128)(2,1)}, u32[]{:S(2)}) copy-start(bf16[4,256,512]{2,1,0:T(8,128)(2,1)} %param.6) | copy-start | bytes 3145732
  6.5 59.7 %all-gather.11.cloned.1.call-start = ((), (), s32[]{:S(2)}) async-start(), calls=%async_computation.2 | async-start | bytes 9437184 | tf_op jit(solution)/shard_map/all_gather | solution.py:44
  7.3 141.3 %all-gather.21.cloned.1.call-start = ((), (), s32[]{:S(2)}) async-start(), calls=%async_computation.9 | async-start | bytes 5242880 | tf_op jit(solution)/shard_map/all_gather | solution.py:57
  8.0 168.8 %all-gather.13.cloned.1.call-start = ((), (), s32[]{:S(2)}) async-start(), calls=%async_computation.4 | async-start | bytes 2359296 | tf_op jit(solution)/shard_map/all_gather | solution.py:68
  8.7 256.4 %all-reduce.4.cloned.1.call-start = ((), (), s32[]{:S(2)}) async-start(), calls=%async_computation.3 | async-start | bytes 4194304 | tf_op jit(solution)/shard_map/psum | solution.py:63
  73.4 238.0 %all-gather.23.cloned.1.call-start = ((), (), s32[]{:S(2)}) async-start(), calls=%async_computation.11 | async-start | bytes 2621440 | tf_op jit(solution)/shard_map/all_gather | solution.py:75
  73.9 320.1 %all-reduce.6.cloned.1.call-start = ((), (), s32[]{:S(2)}) async-start(), calls=%async_computation.10 | async-start | bytes 8388608 | tf_op jit(solution)/shard_map/psum | solution.py:64
  155.2 268.7 %all-gather.15.cloned.1.call-start = ((), (), s32[]{:S(2)}) async-start(), calls=%async_computation.5 | async-start | bytes 2359296 | tf_op jit(solution)/shard_map/all_gather | solution.py:69
  270.0 233.2 %all-gather.25.cloned.1.call-start = ((), (), s32[]{:S(2)}) async-start(), calls=%async_computation.12 | async-start | bytes 2621440 | tf_op jit(solution)/shard_map/all_gather | solution.py:76
  401.2 182.7 %all-gather.17.cloned.1.call-start = ((), (), s32[]{:S(2)}) async-start(), calls=%async_computation.6 | async-start | bytes 2359296 | tf_op jit(solution)/shard_map/all_gather | solution.py:69
  429.5 66.6 %copy-start.7 = (f32[2048,256]{1,0:T(8,128)S(1)}, f32[2048,256]{1,0:T(8,128)}, u32[]{:S(2)}) copy-start(f32[2048,256]{1,0:T(8,128)} %all-gather.15.cloned.1.call-done) | copy-start | bytes 6291460
  431.4 0.7 copy-start.16
  467.8 2.0 copy-start.11
  475.0 0.6 copy-start.21
  497.2 2.9 copy-start.8
  502.8 161.2 %all-gather.27.cloned.1.call-start = ((), (), s32[]{:S(2)}) async-start(), calls=%async_computation.13 | async-start | bytes 2621440 | tf_op jit(solution)/shard_map/all_gather | solution.py:76
  508.9 66.4 %copy-start.2 = (f32[2048,256]{1,0:T(8,128)S(1)}, f32[2048,256]{1,0:T(8,128)}, u32[]{:S(2)}) copy-start(f32[2048,256]{1,0:T(8,128)} %all-gather.25.cloned.1.call-done) | copy-start | bytes 6291460
  510.8 0.7 copy-start.17
  547.1 1.9 copy-start.12
  554.2 0.7 copy-start.22
  576.4 2.9 copy-start
  583.7 161.7 %all-gather.19.cloned.1.call-start = ((), (), s32[]{:S(2)}) async-start(), calls=%async_computation.7 | async-start | bytes 2359296 | tf_op jit(solution)/shard_map/all_gather | solution.py:69
  589.7 67.5 %copy-start.3 = (f32[2048,256]{1,0:T(8,128)S(1)}, f32[2048,256]{1,0:T(8,128)}, u32[]{:S(2)}) copy-start(f32[2048,256]{1,0:T(8,128)} %all-gather.17.cloned.1.call-done) | copy-start | bytes 6291460
  591.5 0.7 copy-start.18
  628.8 2.0 copy-start.13
  636.0 0.6 copy-start.23
  658.2 2.9 copy-start.9
  663.8 160.4 %all-gather.29.cloned.1.call-start = ((), (), s32[]{:S(2)}) async-start(), calls=%async_computation.14 | async-start | bytes 2621440 | tf_op jit(solution)/shard_map/all_gather | solution.py:76
  669.7 66.8 %copy-start.5 = (f32[2048,256]{1,0:T(8,128)S(1)}, f32[2048,256]{1,0:T(8,128)}, u32[]{:S(2)}) copy-start(f32[2048,256]{1,0:T(8,128)} %all-gather.27.cloned.1.call-done) | copy-start | bytes 6291460
  671.5 0.7 copy-start.19
  708.6 1.8 copy-start.14
  715.4 0.7 copy-start.24
  737.6 2.9 copy-start.1
  744.9 149.6 %reduce-scatter.5.cloned.1.call-start = ((), (), s32[]{:S(2)}) async-start(), calls=%async_computation.8 | async-start | bytes 2359296 | tf_op jit(solution)/shard_map/reduce_scatter | solution.py:82
  751.0 67.0 %copy-start.6 = (f32[2048,256]{1,0:T(8,128)S(1)}, f32[2048,256]{1,0:T(8,128)}, u32[]{:S(2)}) copy-start(f32[2048,256]{1,0:T(8,128)} %all-gather.19.cloned.1.call-done) | copy-start | bytes 6291460
  752.9 0.7 copy-start.20
  789.9 2.0 copy-start.15
  796.9 0.7 copy-start.25
  823.9 92.7 %reduce-scatter.7.cloned.1.call-start = ((), (), s32[]{:S(2)}) async-start(), calls=%async_computation.15 | async-start | bytes 163840
  829.8 60.6 %copy-start.4 = (f32[2048,256]{1,0:T(8,128)S(1)}, f32[2048,256]{1,0:T(8,128)}, u32[]{:S(2)}) copy-start(f32[2048,256]{1,0:T(8,128)} %all-gather.29.cloned.1.call-done) | copy-start | bytes 6291460
Sparse Core Ops, SparseCore 0:
  9.2 56.9 all-gather.10
  67.8 80.7 all-gather.20
  150.5 26.2 all-gather.12
  179.0 86.1 all-reduce.3
  266.6 44.6 all-gather.22
  314.4 79.5 all-reduce.5
  396.0 27.8 all-gather.14
  425.4 45.6 all-gather.24
  502.9 27.8 all-gather.16
  583.8 45.6 all-gather.26
  663.9 27.8 all-gather.18
  745.0 45.6 all-gather.28
  824.0 41.2 reduce-scatter.4
  897.1 19.3 reduce-scatter.6
where the time goes:
time: 934 us; the launch traced here: 925 us
  waiting for transfers between devices  411 us (44%)
  other arithmetic  340 us (36%)
  matrix products  112 us (12%)
  local copies, waits for them, and re-layouts  38.1 us (4%)
  between operations  22.2 us (2%)
    another operation x40, other arithmetic, orth_rows(): lower = jnp.linalg.cholesky(inner)  208 us
    another operation x13, other arithmetic, orth_rows(): lax.linalg.triangular_solve(lower, image, left_side=False, lower=True, tr...  127 us
    psum x1, waiting for transfers between devices, on_device(): gram_x = lax.psum(partial_x, 'gy')  88.4 us
    psum x1, waiting for transfers between devices, on_device(): gram_y = lax.psum(partial_y, 'gx')  82.8 us
    all_gather x1, waiting for transfers between devices, gram_rows_y(): lax.all_gather(history, 'gy', axis=2, tiled=True)  74.6 us
    all_gather x1, waiting for transfers between devices, gram_rows_x(): lax.all_gather(history, 'gx', axis=1, tiled=True)  57.5 us
    all_gather x1, waiting for transfers between devices, on_device(): lax.all_gather(local, 'gy', axis=0, tiled=True)  41.3 us
    dot_general x6, matrix products, self_inner(): jnp.dot(image.T, image, precision=lax.Precision.HIGHEST, preferred_elemen...  34.1 us
  transfers between devices with their start and end apart: 14, of which 8 were waited for; matrix products, arithmetic and copies ran while one was open for 52% of the time, Pallas kernels for 0%

commit v1 on v0

v1 whole, which is shorter than its diff:
```python
import functools

import jax
import jax.numpy as jnp
from jax import lax
from jax.experimental import pallas as pl
from jax.experimental.pallas import tpu as pltpu
from jax.sharding import PartitionSpec as P

ITERS = 3
BLOCK = 64
HIGH = lax.Precision.HIGH
HIGHEST = lax.Precision.HIGHEST


def eliminate(blocks):
    size = blocks[0].shape[0]
    sub = lax.broadcasted_iota(jnp.int32, (size, size), 0)
    lane = lax.broadcasted_iota(jnp.int32, (size, size), 1)
    eye = jnp.where(sub == lane, 1.0, 0.0).astype(jnp.float32)
    sub8 = lax.broadcasted_iota(jnp.int32, (8, 1), 0)
    tiles = []
    for block in blocks:
        whole = jnp.concatenate([block, eye], axis=1)
        tiles.append([whole[t * 8 : t * 8 + 8] for t in range(size // 8)])
    for k in range(size):
        home = k // 8
        for rows in tiles:
            held = rows[home]
            row = held[k % 8 : k % 8 + 1, :]
            scaled = row / row[:, k : k + 1]
            for t in range(home, size // 8):
                if t == home and k % 8 == 7:
                    continue
                col = rows[t][:, k : k + 1]
                if t == home:
                    col = jnp.where(sub8 > k % 8, col, 0.0)
                rows[t] = rows[t] - col * scaled
    out = []
    for rows in tiles:
        whole = jnp.concatenate(rows, axis=0)
        diag = jnp.sum(jnp.where(sub == lane, whole[:, :size], 0.0), axis=1, keepdims=True)
        out.append(whole[:, size:] * (1.0 / jnp.sqrt(diag)))
    return out


def mul(a, b, dims):
    return lax.dot_general(a, b, (dims, ((), ())), precision=HIGHEST, preferred_element_type=jnp.float32)


def factor_kernel(inner_ref, out_ref, work):
    modes, rank = inner_ref.shape[0], inner_ref.shape[1]
    sub = lax.broadcasted_iota(jnp.int32, (rank, rank), 0)
    lane = lax.broadcasted_iota(jnp.int32, (rank, rank), 1)
    eye = jnp.where(sub == lane, 1.0, 0.0).astype(jnp.float32)
    for m in range(modes):
        work[m, :, :rank] = inner_ref[m]
        work[m, :, rank:] = eye
    for p in range(rank // BLOCK):
        at = p * BLOCK
        inverses = eliminate([work[m, at : at + BLOCK, at : at + BLOCK] for m in range(modes)])
        for m in range(modes):
            top = mul(inverses[m], work[m, at : at + BLOCK, :], ((1,), (0,)))
            out_ref[m, at : at + BLOCK, :] = top[:, rank:]
            if at + BLOCK < rank:
                left = top[:, at + BLOCK : rank]
                work[m, at + BLOCK :, :] = work[m, at + BLOCK :, :] - mul(left, top, ((0,), (0,)))


def inverse_factors(inner):
    modes, rank = inner.shape[0], inner.shape[1]
    return pl.pallas_call(
        factor_kernel,
        out_shape=jax.ShapeDtypeStruct(inner.shape, jnp.float32),
        in_specs=[pl.BlockSpec(memory_space=pltpu.VMEM)],
        out_specs=pl.BlockSpec(memory_space=pltpu.VMEM),
        scratch_shapes=[pltpu.VMEM((modes, rank, 2 * rank), jnp.float32)],
        name="inverse_factors",
    )(inner)


def dot(a, b, precision):
    return jnp.dot(a, b, precision=precision, preferred_element_type=jnp.float32)


def on_device(history, start_x, start_y):
    nx, ny = lax.axis_size("gx"), lax.axis_size("gy")
    rows, cols, rank = history.shape[1], history.shape[2], start_x.shape[1]
    basis_x = lax.all_gather(start_x, "gx", axis=0, tiled=True)
    basis_y = lax.all_gather(start_y, "gy", axis=0, tiled=True)
    gram_x = lax.dot_general(
        history, lax.all_gather(history, "gx", axis=1, tiled=True),
        (((0, 2), (0, 2)), ((), ())), preferred_element_type=jnp.float32,
    )
    gram_y = lax.dot_general(
        history, lax.all_gather(history, "gy", axis=2, tiled=True),
        (((0, 1), (0, 1)), ((), ())), preferred_element_type=jnp.float32,
    )
    for step in range(ITERS):
        part_x = lax.psum_scatter(dot(gram_x, basis_x, HIGH), "gy", scatter_dimension=0, tiled=True)
        part_y = lax.psum_scatter(dot(gram_y, basis_y, HIGH), "gx", scatter_dimension=0, tiled=True)
        both = jnp.stack([part_x, part_y])
        both = lax.all_gather(both, "gy", axis=1)
        both = lax.all_gather(both, "gx", axis=1)
        image_x = both[0].reshape(-1, rank)
        image_y = both[1].swapaxes(0, 1).reshape(-1, rank)
        inner = jnp.stack([dot(image_x.T, image_x, HIGHEST), dot(image_y.T, image_y, HIGHEST)])
        inverse = inverse_factors(inner)
        if step == ITERS - 1:
            image_x = lax.dynamic_slice_in_dim(image_x, lax.axis_index("gx") * rows, rows, 0)
            image_y = lax.dynamic_slice_in_dim(image_y, lax.axis_index("gy") * cols, cols, 0)
        basis_x = dot(image_x, inverse[0].T, HIGH)
        basis_y = dot(image_y, inverse[1].T, HIGH)
    factor_x = basis_x.astype(jnp.bfloat16)
    factor_y = basis_y.astype(jnp.bfloat16)
    first = jnp.einsum("xa,sxy->say", factor_x, history, preferred_element_type=jnp.float32)
    first = lax.psum_scatter(first, "gx", scatter_dimension=1, tiled=True)
    second = jnp.einsum("say,yb->sab", first, factor_y.astype(jnp.float32), precision=HIGHEST)
    return lax.psum_scatter(second, "gy", scatter_dimension=2, tiled=True)


def solution(mesh):
    return jax.shard_map(
        on_device,
        mesh=mesh,
        in_specs=(P(None, "gx", "gy"), P("gx", None), P("gy", None)),
        out_specs=P(None, "gx", "gy"),
        check_vma=False,
    )
```

time: 934 us -> 761 us (0.81)
  other arithmetic: 340 us -> 5.18 us
  waiting for transfers between devices: 411 us -> 523 us
  Pallas kernels: 0 us -> 83.4 us
  blocking collectives: 0 us -> 48.2 us
  matrix products: 112 us -> 64.5 us
  local copies, waits for them, and re-layouts: 38.1 us -> 14.8 us
    another operation x53 -> x6, other arithmetic: 335 us -> 5.18 us  [the longest x3 2.64 us: on_device(): both = jnp.stack([part_x, part_y])]
    psum x2 -> x0, waiting for transfers between devices: 171 us -> none  [the longest x1 88.4 us: on_device(): gram_x = lax.psum(partial_x, 'gy')]
    reduce_scatter x0 -> x6, waiting for transfers between devices: none -> 157 us  [the longest x3 104 us: on_device(): lax.psum_scatter(dot(gram_y, basis_y, HIGH), 'gx', scatter_dimension=0, t...]
    all_gather x10 -> x7, waiting for transfers between devices: 217 us -> 305 us  [the longest x3 109 us: on_device(): both = lax.all_gather(both, 'gx', axis=1)]
    pallas_call x0 -> x3, Pallas kernels: none -> 83.4 us  [inverse_factors(): pl.pallas_call(factor_kernel, out_shape=jax.ShapeDtypeStruct(inner.shape,...]
    all_gather x0 -> x3, blocking collectives: none -> 48.2 us  [on_device(): both = lax.all_gather(both, 'gy', axis=1)]
    reduce_scatter x1, waiting for transfers between devices: 0.02 us -> 39.7 us  [on_device(): first = lax.psum_scatter(first, 'gx', scatter_dimension=1, tiled=True)]
    another operation x30 -> x0, matrix products: 35.1 us -> none  [the longest x18 23.9 us: orth_rows(): lax.linalg.triangular_solve(lower, image, left_side=False, lower=True, tr...]
  transfers between devices with their start and end apart: 14 -> 15, of which waited for: 8 -> 15; matrix products, arithmetic and copies ran while one was open for 52% -> 4% of each run, Pallas kernels for 0% -> 0%
where the time goes in v1:
time: 761 us; the launch traced here: 754 us
  waiting for transfers between devices  523 us (69%)
  Pallas kernels  83.4 us (11%)
  matrix products  64.5 us (8%)
  blocking collectives  48.2 us (6%)
  local copies, waits for them, and re-layouts  14.8 us (2%)
  between operations  13.8 us (2%)
    all_gather x3, waiting for transfers between devices, on_device(): both = lax.all_gather(both, 'gx', axis=1)  109 us
    reduce_scatter x3, waiting for transfers between devices, on_device(): lax.psum_scatter(dot(gram_y, basis_y, HIGH), 'gx', scatter_dimension=0, t...  104 us
    pallas_call x3, Pallas kernels, inverse_factors(): pl.pallas_call(factor_kernel, out_shape=jax.ShapeDtypeStruct(inner.shape,...  83.4 us
    all_gather x1, waiting for transfers between devices, on_device(): lax.all_gather(history, 'gy', axis=2, tiled=True)  83 us
    reduce_scatter x3, waiting for transfers between devices, on_device(): lax.psum_scatter(dot(gram_x, basis_x, HIGH), 'gy', scatter_dimension=0, t...  52.2 us
    all_gather x1, waiting for transfers between devices, on_device(): lax.all_gather(history, 'gx', axis=1, tiled=True)  49.4 us
    dot_general x18, matrix products, dot(): jnp.dot(a, b, precision=precision, preferred_element_type=jnp.float32)  49.2 us
    all_gather x3, blocking collectives, on_device(): both = lax.all_gather(both, 'gy', axis=1)  48.2 us
  transfers between devices with their start and end apart: 15, of which 15 were waited for; matrix products, arithmetic and copies ran while one was open for 4% of the time, Pallas kernels for 0%

profile of v1, /device:TPU:0, one launch (start us, length us, event | category | flops | bytes accessed | tf_op | source)
XLA Modules:
  0.0 754.4 jit_solution(8317916846639689542)
XLA Ops:
  6.5 0.7 all-gather.18.cloned.1.call-update
  7.3 0.7 all-gather.20.cloned.1.call-update
  8.1 0.7 all-gather.14.cloned.1.call-update
  8.8 0.5 all-gather.16.cloned.1.call-update
  9.4 83.0 %all-gather.18.cloned.1.call-done = bf16[4,256,2048]{2,1,0:T(8,128)(2,1)} async-done(((bf16[4,256,512]{2,1,0:T(8,128)(2,1)}), bf16[4,256,2048]{2,1,0:T(8,128)(2,1)}) %all-gather.18.cloned.1.call-update) | async-done | bytes 4194320 | tf_op jit(solution)/shard_map/all_gather | solution.py:96
  92.4 6.6 fusion.38
  99.0 39.2 %all-gather.20.cloned.1.call-done = f32[2048,256]{1,0:T(8,128)} async-done(((f32[512,256]{1,0:T(8,128)}), f32[2048,256]{1,0:T(8,128)}) %all-gather.20.cloned.1.call-update) | async-done | bytes 2097168 | tf_op jit(solution)/shard_map/all_gather | solution.py:90
  138.1 5.5 fusion.4
  143.7 49.4 %all-gather.14.cloned.1.call-done = bf16[4,2048,512]{2,1,0:T(8,128)(2,1)} async-done(((bf16[4,256,512]{2,1,0:T(8,128)(2,1)}), bf16[4,2048,512]{2,1,0:T(8,128)(2,1)}) %all-gather.14.cloned.1.call-update) | async-done | bytes 8388624 | tf_op jit(solution)/shard_map/all_gather | solution.py:92
  193.2 5.7 convolution_bitcast_fusion
  198.9 23.8 %all-gather.16.cloned.1.call-done = f32[2048,256]{1,0:T(8,128)} async-done(((f32[256,256]{1,0:T(8,128)}), f32[2048,256]{1,0:T(8,128)}) %all-gather.16.cloned.1.call-update) | async-done | bytes 2097168 | tf_op jit(solution)/shard_map/all_gather | solution.py:89
  222.7 3.4 fusion.37
  226.1 33.6 %reduce-scatter.13.cloned.1.call-done = f32[64,256]{1,0:T(8,128)} async-done(((f32[512,256]{1,0:T(8,128)}), f32[64,256]{1,0:T(8,128)}) %reduce-scatter.13.cloned.1.call-update) | async-done | bytes 65552 | tf_op jit(solution)/shard_map/reduce_scatter | solution.py:101
  259.8 22.1 %reduce-scatter.11.cloned.1.call-done = f32[64,256]{1,0:T(8,128)} async-done(((f32[256,256]{1,0:T(8,128)}), f32[64,256]{1,0:T(8,128)}) %reduce-scatter.11.cloned.1.call-update) | async-done | bytes 65552 | tf_op jit(solution)/shard_map/reduce_scatter | solution.py:100
  281.9 0.9 pad_maximum_fusion.3
  282.8 15.9 %all-gather = f32[2,256,256]{2,1,0:T(8,128)} all-gather(f32[2,64,256]{2,1,0:T(8,128)S(1)} %pad_maximum_fusion.3), channel_id=2, replica_groups=mesh['gx'=8,'gy'=4] {'gy'}, dimensions={1}, use_global_device_ids=true | all-gather | bytes 655360 | tf_op jit(solution)/shard_map/all_gather | solution.py:103
  298.7 0.3 reduce-scatter.15.cloned.1.call-start
  299.0 34.7 %all-gather.22.cloned.1.call-done = f32[2,32,64,256]{3,2,1,0:T(8,128)} async-done(((f32[2,4,64,256]{3,2,1,0:T(8,128)}), f32[2,32,64,256]{3,2,1,0:T(8,128)}) %all-gather.22.cloned.1.call-update) | async-done | bytes 4194320 | tf_op jit(solution)/shard_map/all_gather | solution.py:104
  333.7 2.5 fusion.36
  336.3 3.5 fusion.13
  339.8 1.6 copy.10
  341.3 3.5 convolution_bitcast_fusion.4
  344.8 0.8 pad_maximum_fusion.inner_ref
  345.7 28.0 %inverse_factors.3 = f32[2,256,256]{2,1,0:T(8,128)} custom-call(f32[2,256,256]{2,1,0:T(8,128)} %pad_maximum_fusion.inner_ref), custom_call_target="tpu_custom_call" | custom-call | tf_op jit(solution)/shard_map/inverse_factors/pallas_call | solution.py:72
  373.7 2.1 fusion.27
  375.8 1.9 fusion.39
  377.8 2.1 fusion.26
  380.0 2.7 fusion.2
  382.8 15.0 %reduce-scatter.15.cloned.1.call-done = f32[64,256]{1,0:T(8,128)} async-done(((f32[256,256]{1,0:T(8,128)}), f32[64,256]{1,0:T(8,128)}) %reduce-scatter.15.cloned.1.call-update) | async-done | bytes 65552 | tf_op jit(solution)/shard_map/reduce_scatter | solution.py:100
  397.9 35.5 %reduce-scatter.17.cloned.1.call-done = f32[64,256]{1,0:T(8,128)} async-done(((f32[512,256]{1,0:T(8,128)}), f32[64,256]{1,0:T(8,128)}) %reduce-scatter.17.cloned.1.call-update) | async-done | bytes 65552 | tf_op jit(solution)/shard_map/reduce_scatter | solution.py:101
  433.3 0.9 pad_maximum_fusion.4
  434.2 16.1 %all-gather.2 = f32[2,256,256]{2,1,0:T(8,128)} all-gather(f32[2,64,256]{2,1,0:T(8,128)S(1)} %pad_maximum_fusion.4), channel_id=4, replica_groups=mesh['gx'=8,'gy'=4] {'gy'}, dimensions={1}, use_global_device_ids=true | all-gather | bytes 655360 | tf_op jit(solution)/shard_map/all_gather | solution.py:103
  450.6 37.4 %all-gather.24.cloned.1.call-done = f32[2,32,64,256]{3,2,1,0:T(8,128)} async-done(((f32[2,4,64,256]{3,2,1,0:T(8,128)}), f32[2,32,64,256]{3,2,1,0:T(8,128)}) %all-gather.24.cloned.1.call-update) | async-done | bytes 4194320 | tf_op jit(solution)/shard_map/all_gather | solution.py:104
  488.0 2.5 fusion.35
  490.5 3.5 fusion.16
  494.0 1.6 copy.11
  495.5 3.5 convolution_bitcast_fusion.3
  499.0 0.8 pad_maximum_fusion.1.inner_ref
  499.9 27.7 %inverse_factors.4 = f32[2,256,256]{2,1,0:T(8,128)} custom-call(f32[2,256,256]{2,1,0:T(8,128)} %pad_maximum_fusion.1.inner_ref), custom_call_target="tpu_custom_call" | custom-call | tf_op jit(solution)/shard_map/inverse_factors/pallas_call | solution.py:72
  527.6 2.1 fusion.25
  529.7 1.9 fusion.40
  531.7 2.1 fusion.24
  533.9 2.7 fusion
  536.7 15.1 %reduce-scatter.19.cloned.1.call-done = f32[64,256]{1,0:T(8,128)} async-done(((f32[256,256]{1,0:T(8,128)}), f32[64,256]{1,0:T(8,128)}) %reduce-scatter.19.cloned.1.call-update) | async-done | bytes 65552 | tf_op jit(solution)/shard_map/reduce_scatter | solution.py:100
  551.8 35.2 %reduce-scatter.21.cloned.1.call-done = f32[64,256]{1,0:T(8,128)} async-done(((f32[512,256]{1,0:T(8,128)}), f32[64,256]{1,0:T(8,128)}) %reduce-scatter.21.cloned.1.call-update) | async-done | bytes 65552 | tf_op jit(solution)/shard_map/reduce_scatter | solution.py:101
  587.1 0.9 pad_maximum_fusion.5
  587.9 16.2 %all-gather.4 = f32[2,256,256]{2,1,0:T(8,128)} all-gather(f32[2,64,256]{2,1,0:T(8,128)S(1)} %pad_maximum_fusion.5), channel_id=6, replica_groups=mesh['gx'=8,'gy'=4] {'gy'}, dimensions={1}, use_global_device_ids=true | all-gather | bytes 655360 | tf_op jit(solution)/shard_map/all_gather | solution.py:103
  604.1 0.4 reduce-scatter.23.cloned.1.call-start
  604.6 37.1 %all-gather.26.cloned.1.call-done = f32[2,32,64,256]{3,2,1,0:T(8,128)} async-done(((f32[2,4,64,256]{3,2,1,0:T(8,128)}), f32[2,32,64,256]{3,2,1,0:T(8,128)}) %all-gather.26.cloned.1.call-update) | async-done | bytes 4194320 | tf_op jit(solution)/shard_map/all_gather | solution.py:104
  641.7 2.5 fusion.34
  644.2 3.5 convolution_bitcast_fusion.2
  647.7 3.5 fusion.19
  651.2 0.8 pad_maximum_fusion.2.inner_ref
  652.1 27.7 %inverse_factors.5 = f32[2,256,256]{2,1,0:T(8,128)} custom-call(f32[2,256,256]{2,1,0:T(8,128)} %pad_maximum_fusion.2.inner_ref), custom_call_target="tpu_custom_call" | custom-call | tf_op jit(solution)/shard_map/inverse_factors/pallas_call | solution.py:72
  679.7 1.3 fusion.22
  681.0 1.8 convolution_bitcast_fusion.1
  683.1 0.9 copy-done.10
  684.0 0.4 fusion.12
  684.4 39.7 %reduce-scatter.23.cloned.1.call-done = f32[4,32,512]{2,1,0:T(8,128)} async-done(((f32[4,256,512]{2,1,0:T(8,128)}), f32[4,32,512]{2,1,0:T(8,128)}) %reduce-scatter.23.cloned.1.call-update) | async-done | bytes 262160 | tf_op jit(solution)/shard_map/reduce_scatter | solution.py:117
  724.1 1.2 fusion.41
  725.6 0.9 reshape.58
  726.5 19.6 %reduce-scatter.25.cloned.1.call-done = f32[64,128]{1,0:T(8,128)} async-done(((f32[256,128]{1,0:T(8,128)}), f32[64,128]{1,0:T(8,128)}) %reduce-scatter.25.cloned.1.call-update) | async-done | bytes 32784
  746.1 0.9 reshape.59
  747.0 0.7 copy.24
  (47 shorter events, 1.5 us)
Async XLA Ops:
  6.5 85.9 %copy-start.5 = (bf16[4,256,512]{2,1,0:T(8,128)(2,1)S(1)}, bf16[4,256,512]{2,1,0:T(8,128)(2,1)}, u32[]{:S(2)}) copy-start(bf16[4,256,512]{2,1,0:T(8,128)(2,1)} %param.3) | copy-start | bytes 3145732
  6.5 85.9 %all-gather.18.cloned.1.call-start = ((), (), s32[]{:S(2)}) async-start(), calls=%async_computation.11 | async-start | bytes 5242880 | tf_op jit(solution)/shard_map/all_gather | solution.py:96
  7.3 130.9 %all-gather.20.cloned.1.call-start = ((), (), s32[]{:S(2)}) async-start(), calls=%async_computation.12 | async-start | bytes 2621440 | tf_op jit(solution)/shard_map/all_gather | solution.py:90
  8.0 185.1 %all-gather.14.cloned.1.call-start = ((), (), s32[]{:S(2)}) async-start(), calls=%async_computation.8 | async-start | bytes 9437184 | tf_op jit(solution)/shard_map/all_gather | solution.py:92
  8.7 214.0 %all-gather.16.cloned.1.call-start = ((), (), s32[]{:S(2)}) async-start(), calls=%async_computation.9 | async-start | bytes 2359296 | tf_op jit(solution)/shard_map/all_gather | solution.py:89
  9.3 250.4 %reduce-scatter.13.cloned.1.call-start = ((), (), s32[]{:S(2)}) async-start(), calls=%async_computation.13 | async-start | bytes 589824 | tf_op jit(solution)/shard_map/reduce_scatter | solution.py:101
  143.7 138.2 %reduce-scatter.11.cloned.1.call-start = ((), (), s32[]{:S(2)}) async-start(), calls=%async_computation.10 | async-start | bytes 327680 | tf_op jit(solution)/shard_map/reduce_scatter | solution.py:100
  198.9 27.2 %copy-start.2 = (f32[256,2048]{1,0:T(8,128)}, f32[256,2048]{1,0:T(8,128)S(1)}, u32[]{:S(2)}) copy-start(f32[256,2048]{1,0:T(8,128)S(1)} %convolution_bitcast_fusion) | copy-start | bytes 6291460
  226.1 107.6 %all-gather.22.cloned.1.call-start = ((), (), s32[]{:S(2)}) async-start(), calls=%async_computation.19 | async-start | bytes 4718592 | tf_op jit(solution)/shard_map/all_gather | solution.py:104
  298.7 99.2 %reduce-scatter.15.cloned.1.call-start = ((), (), s32[]{:S(2)}) async-start(), calls=%async_computation.14 | async-start | bytes 327680 | tf_op jit(solution)/shard_map/reduce_scatter | solution.py:100
  373.7 2.1 copy-start.3
  375.8 1.9 copy-start.7
  377.7 55.6 %reduce-scatter.17.cloned.1.call-start = ((), (), s32[]{:S(2)}) async-start(), calls=%async_computation.15 | async-start | bytes 589824 | tf_op jit(solution)/shard_map/reduce_scatter | solution.py:101
  377.8 2.3 copy-start
  382.8 105.2 %all-gather.24.cloned.1.call-start = ((), (), s32[]{:S(2)}) async-start(), calls=%async_computation.20 | async-start | bytes 4718592 | tf_op jit(solution)/shard_map/all_gather | solution.py:104
  450.3 101.5 %reduce-scatter.19.cloned.1.call-start = ((), (), s32[]{:S(2)}) async-start(), calls=%async_computation.16 | async-start | bytes 327680 | tf_op jit(solution)/shard_map/reduce_scatter | solution.py:100
  527.6 2.1 copy-start.4
  529.7 1.9 copy-start.6
  531.6 55.4 %reduce-scatter.21.cloned.1.call-start = ((), (), s32[]{:S(2)}) async-start(), calls=%async_computation.17 | async-start | bytes 589824 | tf_op jit(solution)/shard_map/reduce_scatter | solution.py:101
  531.7 2.3 copy-start.1
  536.7 105.0 %all-gather.26.cloned.1.call-start = ((), (), s32[]{:S(2)}) async-start(), calls=%async_computation.21 | async-start | bytes 4718592 | tf_op jit(solution)/shard_map/all_gather | solution.py:104
  604.1 120.0 %reduce-scatter.23.cloned.1.call-start = ((), (), s32[]{:S(2)}) async-start(), calls=%async_computation.18 | async-start | bytes 2359296 | tf_op jit(solution)/shard_map/reduce_scatter | solution.py:117
  644.2 3.5 copy-start.8
  681.0 1.9 copy-start.9
  682.9 63.2 %reduce-scatter.25.cloned.1.call-start = ((), (), s32[]{:S(2)}) async-start(), calls=%async_computation.22 | async-start | bytes 163840
  683.0 1.0 copy-start.10
Sparse Core Ops, SparseCore 0:
  8.9 83.4 all-gather.17
  94.0 44.1 all-gather.19
  140.1 53.0 all-gather.13
  194.9 27.7 all-gather.15
  225.6 34.0 reduce-scatter.12
  261.9 19.9 reduce-scatter.10
  298.8 34.8 all-gather.21
  377.8 19.9 reduce-scatter.14
  400.9 32.3 reduce-scatter.16
  450.5 37.4 all-gather.23
  531.7 20.0 reduce-scatter.18
  554.7 32.2 reduce-scatter.20
  604.3 37.4 all-gather.25
  683.0 41.0 reduce-scatter.22
  726.6 19.4 reduce-scatter.24

commit v2 on v1

--- a/solution.py
+++ b/solution.py
@@ -79,31 +79,263 @@
     )(inner)
 
 
+MESH = pl.DeviceIdType.MESH
+
+
+def send(src, dst, sems, at, device):
+    return pltpu.make_async_remote_copy(
+        src_ref=src, dst_ref=dst, send_sem=sems[0].at[at], recv_sem=sems[1].at[at],
+        device_id=device, device_id_type=MESH,
+    )
+
+
+def greet(nx, ny, i, j):
+    barrier = pltpu.get_barrier_semaphore()
+    for d in range(1, ny):
+        pl.semaphore_signal(barrier, inc=1, device_id=(i, lax.rem(j + d, ny)), device_id_type=MESH)
+    for e in range(1, nx):
+        pl.semaphore_signal(barrier, inc=1, device_id=(lax.rem(i + e, nx), j), device_id_type=MESH)
+    pl.semaphore_wait(barrier, nx + ny - 2)
+
+
+def spread(nx, ny, i, j, outs, rows, sems, between=None):
+    half = nx // 2
+    chip, core = i // 2, lax.rem(i, 2)
+    sibling = (i + 1 - 2 * core, j)
+    line, plane, pair = sems
+
+    def places(ii, jj):
+        spots = (ii * ny + jj, jj * nx + ii)
+        return [outs[m].at[pl.ds(pl.multiple_of(spots[m] * rows, rows), rows), :] for m in range(2)]
+
+    sent = []
+
+    def push(block, group, at, device):
+        for m in range(2):
+            copy = send(block[m], block[m], group, at + (m,), device)
+            copy.start()
+            sent.append(copy)
+
+    def fan(d):
+        jj = lax.rem(j - d + ny, ny)
+        block = places(i, jj)
+        for e in range(1, half):
+            push(block, plane, (e, d), (lax.rem(chip + e, half) * 2 + core, j))
+        push(block, pair, (0, d), sibling)
+
+    for d in range(1, ny):
+        push(places(i, j), line, (d,), (i, lax.rem(j + d, ny)))
+    fan(0)
+    if between is not None:
+        between()
+    for d in range(1, ny):
+        for m, block in enumerate(places(i, lax.rem(j - d + ny, ny))):
+            send(block, block, line, (d, m), sibling).wait_recv()
+        fan(d)
+    for d in range(ny):
+        for e in range(1, half):
+            ii = lax.rem(chip - e + half, half) * 2 + core
+            block = places(ii, lax.rem(j - d + ny, ny))
+            for m in range(2):
+                send(block[m], block[m], plane, (e, d, m), sibling).wait_recv()
+            push(block, pair, (e, d), sibling)
+    other = i + 1 - 2 * core
+
+    def finish():
+        for d in range(ny):
+            for e in range(half):
+                ii = lax.rem(chip - e + half, half) * 2 + (1 - core)
+                block = places(ii, lax.rem(j - d + ny, ny))
+                for m in range(2):
+                    send(block[m], block[m], pair, (e, d, m), sibling).wait_recv()
+        for copy in sent:
+            copy.wait_send()
+
+    return finish
+
+
+def spread_sems(nx, ny):
+    half = nx // 2
+    shapes = []
+    for shape in ((ny, 2), (half, ny, 2), (half, ny, 2)):
+        shapes += [pltpu.SemaphoreType.DMA(shape)] * 2
+    return shapes
+
+
+def exchange_kernel(nx, ny, px_ref, py_ref, ox_ref, oy_ref, sx, sy, xs, xr, ys, yr, ls, lr, ps, pr, bs, br):
+    i, j = lax.axis_index("gx"), lax.axis_index("gy")
+    rows = px_ref.shape[0] // ny
+    greet(nx, ny, i, j)
+
+    def part(ref, at):
+        return ref.at[pl.ds(pl.multiple_of(at * rows, rows), rows), :]
+
+    copies_x, copies_y = [], []
+    for e in range(1, nx):
+        to = lax.rem(i + e, nx)
+        copies_y.append(send(part(py_ref, to), sy.at[e - 1], (ys, yr), e - 1, (to, j)))
+    for d in range(1, ny):
+        to = lax.rem(j + d, ny)
+        copies_x.append(send(part(px_ref, to), sx.at[d - 1], (xs, xr), d - 1, (i, to)))
+    for copy in copies_x + copies_y:
+        copy.start()
+    for copy in copies_x:
+        copy.wait_recv()
+    total = part(px_ref, j)[...]
+    for d in range(1, ny):
+        total = total + sx[d - 1]
+    part(ox_ref, i * ny + j)[...] = total
+    for copy in copies_y:
+        copy.wait_recv()
+    total = part(py_ref, i)[...]
+    for e in range(1, nx):
+        total = total + sy[e - 1]
+    part(oy_ref, j * nx + i)[...] = total
+    finish = spread(nx, ny, i, j, (ox_ref, oy_ref), rows, ((ls, lr), (ps, pr), (bs, br)))
+    finish()
+    for copy in copies_x + copies_y:
+        copy.wait_send()
+
+
+def exchange(nx, ny, part_x, part_y):
+    rows, rank = part_x.shape[0] // ny, part_x.shape[1]
+    whole = jax.ShapeDtypeStruct((rows * nx * ny, rank), jnp.float32)
+    dma = pltpu.SemaphoreType.DMA
+    return pl.pallas_call(
+        functools.partial(exchange_kernel, nx, ny),
+        out_shape=(whole, whole),
+        in_specs=[pl.BlockSpec(memory_space=pltpu.VMEM)] * 2,
+        out_specs=[pl.BlockSpec(memory_space=pltpu.VMEM)] * 2,
+        scratch_shapes=[
+            pltpu.VMEM((ny - 1, rows, rank), jnp.float32),
+            pltpu.VMEM((nx - 1, rows, rank), jnp.float32),
+            dma((ny - 1,)), dma((ny - 1,)), dma((nx - 1,)), dma((nx - 1,)),
+        ] + spread_sems(nx, ny),
+        compiler_params=pltpu.CompilerParams(collective_id=0, has_side_effects=True),
+        name="exchange",
+    )(part_x, part_y)
+
+
+def gather_kernel(nx, ny, h_ref, bx_ref, by_ref, hx_ref, hy_ref, ox_ref, oy_ref, own, gs, gr, fs, fr, ks, hs_r, hs_l, hr, ls, lr, ps, pr, bs, br):
+    i, j = lax.axis_index("gx"), lax.axis_index("gy")
+    half = nx // 2
+    chip, core = i // 2, lax.rem(i, 2)
+    other = i + 1 - 2 * core
+    sibling = (other, j)
+    rows = bx_ref.shape[0]
+    greet(nx, ny, i, j)
+    keep_x = pltpu.make_async_copy(h_ref, hx_ref.at[i], own.at[0])
+    keep_y = pltpu.make_async_copy(h_ref, hy_ref.at[j], own.at[1])
+    begin_x = pltpu.make_async_copy(bx_ref, ox_ref.at[pl.ds(pl.multiple_of((i * ny + j) * rows, rows), rows), :], own.at[2])
+    begin_y = pltpu.make_async_copy(by_ref, oy_ref.at[pl.ds(pl.multiple_of((j * nx + i) * rows, rows), rows), :], own.at[3])
+    for copy in (begin_x, begin_y):
+        copy.start()
+    for copy in (begin_x, begin_y):
+        copy.wait()
+    waits = []
+
+    def right(src, s):
+        return send(src, hy_ref.at[s], (hs_r, hr), s, (i, jnp.minimum(j + 1, ny - 1)))
+
+    def left(src, s):
+        return send(src, hy_ref.at[s], (hs_l, hr), s, (i, jnp.maximum(j - 1, 0)))
+
+    def history():
+        pl.when(j < ny - 1)(lambda: right(h_ref, j).start())
+        pl.when(j > 0)(lambda: left(h_ref, j).start())
+        for e in range(1, half):
+            copy = send(h_ref, hx_ref.at[i], (gs, gr), e, (lax.rem(chip + e, half) * 2 + core, j))
+            copy.start()
+            waits.append(copy)
+        copy = send(h_ref, hx_ref.at[i], (fs, fr), 0, sibling)
+        copy.start()
+        waits.append(copy)
+        keep_x.start()
+        keep_y.start()
+
+    finish = spread(nx, ny, i, j, (ox_ref, oy_ref), rows, ((ls, lr), (ps, pr), (bs, br)), history)
+    for d in range(1, ny):
+        @pl.when(j - d >= 0)
+        def _():
+            s = jnp.maximum(j - d, 0)
+            right(hy_ref.at[s], s).wait_recv()
+            pl.when(j < ny - 1)(lambda: right(hy_ref.at[s], s).start())
+
+        @pl.when(j + d < ny)
+        def _():
+            s = jnp.minimum(j + d, ny - 1)
+            left(hy_ref.at[s], s).wait_recv()
+            pl.when(j > 0)(lambda: left(hy_ref.at[s], s).start())
+    for e in range(1, half):
+        ii = lax.rem(chip - e + half, half) * 2 + core
+        send(hx_ref.at[ii], hx_ref.at[ii], (gs, gr), e, sibling).wait_recv()
+        copy = send(hx_ref.at[ii], hx_ref.at[ii], (fs, fr), e, sibling)
+        copy.start()
+        waits.append(copy)
+    for e in range(half):
+        ii = lax.rem(chip - e + half, half) * 2 + (1 - core)
+        send(hx_ref.at[ii], hx_ref.at[ii], (fs, fr), e, sibling).wait_recv()
+    finish()
+    for copy in waits:
+        copy.wait_send()
+    for d in range(ny):
+        @pl.when(jnp.logical_and(j - d >= 0, j < ny - 1))
+        def _():
+            s = jnp.maximum(j - d, 0)
+            right(hy_ref.at[s], s).wait_send()
+
+        @pl.when(jnp.logical_and(j + d < ny, j > 0))
+        def _():
+            s = jnp.minimum(j + d, ny - 1)
+            left(hy_ref.at[s], s).wait_send()
+    keep_x.wait()
+    keep_y.wait()
+
+
+def gather(nx, ny, history, block_x, block_y):
+    rows, rank = block_x.shape
+    half = nx // 2
+    whole = jax.ShapeDtypeStruct((rows * nx * ny, rank), jnp.float32)
+    dma = pltpu.SemaphoreType.DMA
+    vmem, anywhere = pl.BlockSpec(memory_space=pltpu.VMEM), pl.BlockSpec(memory_space=pl.ANY)
+    return pl.pallas_call(
+        functools.partial(gather_kernel, nx, ny),
+        out_shape=(
+            jax.ShapeDtypeStruct((nx,) + history.shape, history.dtype),
+            jax.ShapeDtypeStruct((ny,) + history.shape, history.dtype),
+            whole, whole,
+        ),
+        in_specs=[vmem] * 3,
+        out_specs=[anywhere, anywhere, vmem, vmem],
+        scratch_shapes=[
+            dma((4,)), dma((half,)), dma((half,)), dma((half,)), dma((half,)),
+            dma((1,)), dma((ny,)), dma((ny,)), dma((ny,)),
+        ] + spread_sems(nx, ny),
+        compiler_params=pltpu.CompilerParams(collective_id=1, has_side_effects=True),
+        name="gather",
+    )(history, block_x, block_y)
+
+
 def dot(a, b, precision):
     return jnp.dot(a, b, precision=precision, preferred_element_type=jnp.float32)
 
 
 def on_device(history, start_x, start_y):
     nx, ny = lax.axis_size("gx"), lax.axis_size("gy")
+    i, j = lax.axis_index("gx"), lax.axis_index("gy")
     rows, cols, rank = history.shape[1], history.shape[2], start_x.shape[1]
-    basis_x = lax.all_gather(start_x, "gx", axis=0, tiled=True)
-    basis_y = lax.all_gather(start_y, "gy", axis=0, tiled=True)
+    share = rows // ny
+    block_x = lax.dynamic_slice_in_dim(start_x, j * share, share, 0)
+    block_y = lax.dynamic_slice_in_dim(start_y, i * share, share, 0)
+    whole_x, whole_y, basis_x, basis_y = gather(nx, ny, history, block_x, block_y)
     gram_x = lax.dot_general(
-        history, lax.all_gather(history, "gx", axis=1, tiled=True),
-        (((0, 2), (0, 2)), ((), ())), preferred_element_type=jnp.float32,
-    )
+        history, whole_x, (((0, 2), (1, 3)), ((), ())), preferred_element_type=jnp.float32
+    ).reshape(rows, nx * rows)
     gram_y = lax.dot_general(
-        history, lax.all_gather(history, "gy", axis=2, tiled=True),
-        (((0, 1), (0, 1)), ((), ())), preferred_element_type=jnp.float32,
-    )
+        history, whole_y, (((0, 1), (1, 2)), ((), ())), preferred_element_type=jnp.float32
+    ).reshape(cols, ny * cols)
     for step in range(ITERS):
-        part_x = lax.psum_scatter(dot(gram_x, basis_x, HIGH), "gy", scatter_dimension=0, tiled=True)
-        part_y = lax.psum_scatter(dot(gram_y, basis_y, HIGH), "gx", scatter_dimension=0, tiled=True)
-        both = jnp.stack([part_x, part_y])
-        both = lax.all_gather(both, "gy", axis=1)
-        both = lax.all_gather(both, "gx", axis=1)
-        image_x = both[0].reshape(-1, rank)
-        image_y = both[1].swapaxes(0, 1).reshape(-1, rank)
+        image_x, image_y = exchange(nx, ny, dot(gram_x, basis_x, HIGH), dot(gram_y, basis_y, HIGH))
         inner = jnp.stack([dot(image_x.T, image_x, HIGHEST), dot(image_y.T, image_y, HIGHEST)])
         inverse = inverse_factors(inner)
         if step == ITERS - 1:

time: 761 us -> 510 us (0.67)
  waiting for transfers between devices: 523 us -> 60 us
  Pallas kernels: 83.4 us -> 340 us
  blocking collectives: 48.2 us -> 0 us
  matrix products: 64.5 us -> 76.6 us
  local copies, waits for them, and re-layouts: 14.8 us -> 6.94 us
    all_gather x7 -> x0, waiting for transfers between devices: 305 us -> none  [the longest x3 109 us: on_device(): both = lax.all_gather(both, 'gx', axis=1)]
    pallas_call x0 -> x4, Pallas kernels: none -> 257 us  [the longest x1 133 us: gather(): pl.pallas_call(functools.partial(gather_kernel, nx, ny), out_shape=(jax.S...]
    reduce_scatter x6 -> x0, waiting for transfers between devices: 157 us -> none  [the longest x3 104 us: on_device(): lax.psum_scatter(dot(gram_y, basis_y, HIGH), 'gx', scatter_dimension=0, t...]
    all_gather x3 -> x0, blocking collectives: 48.2 us -> none  [on_device(): both = lax.all_gather(both, 'gy', axis=1)]
    dot_general x18, matrix products: 49.2 us -> 65 us  [dot(): jnp.dot(a, b, precision=precision, preferred_element_type=jnp.float32)]
    unnamed x16 -> x3, waiting for transfers between devices: 22.4 us -> 19.7 us
  transfers between devices with their start and end apart: 15 -> 2, of which waited for: 15 -> 2; matrix products, arithmetic and copies ran while one was open for 4% -> 0% of each run, Pallas kernels for 0% -> 0%
where the time goes in v2:
time: 510 us; the launch traced here: 500 us
  Pallas kernels  340 us (67%)
  matrix products  76.6 us (15%)
  waiting for transfers between devices  60 us (12%)
  between operations  13.9 us (3%)
  local copies, waits for them, and re-layouts  6.94 us (1%)
    pallas_call x1, Pallas kernels, gather(): pl.pallas_call(functools.partial(gather_kernel, nx, ny), out_shape=(jax.S...  133 us
    pallas_call x3, Pallas kernels, exchange(): pl.pallas_call(functools.partial(exchange_kernel, nx, ny), out_shape=(who...  124 us
    pallas_call x3, Pallas kernels, inverse_factors(): pl.pallas_call(factor_kernel, out_shape=jax.ShapeDtypeStruct(inner.shape,...  83.2 us
    dot_general x18, matrix products, dot(): jnp.dot(a, b, precision=precision, preferred_element_type=jnp.float32)  65 us
    reduce_scatter x1, waiting for transfers between devices, on_device(): first = lax.psum_scatter(first, 'gx', scatter_dimension=1, tiled=True)  40.3 us
    unnamed x3, waiting for transfers between devices  19.7 us
  transfers between devices with their start and end apart: 2, of which 2 were waited for; matrix products, arithmetic and copies ran while one was open for 0% of the time, Pallas kernels for 0%

profile of v2, /device:TPU:0, one launch (start us, length us, event | category | flops | bytes accessed | tf_op | source)
XLA Modules:
  0.0 500.3 jit_solution(4718167863846444122)
XLA Ops:
  6.5 0.0 reduce-scatter.5.cloned.1.call-start
  6.5 1.5 constant_dynamic-slice_fusion
  8.1 132.6 %gather.1 = (bf16[8,4,256,512]{3,2,1,0:T(8,128)(2,1)}, bf16[4,4,256,512]{3,2,1,0:T(8,128)(2,1)}, f32[2048,256]{1,0:T(8,128)}, f32[2048,256]{1,0:T(8,128)}) custom-call(bf16[4,256,512]{2,1,0:T(8,128)(2,1)} %h_ref.1, f32[64,256]{1,0:T(8,128)} %get-tuple-element.26.bx_ref, f32[64,256]{1,0:T(8,128)} %get-tuple-element.25.by_ref), custom_call_target="tpu_custom_call" | custom-call | tf_op jit(solution)/shard_map/gather/pallas_call | solution.py:301
  140.6 0.0 copy-start.8
  140.7 0.0 copy-start.14
  140.7 6.1 %fusion.4 = f32[8,256,256,1]{2,1,3,0:T(8,128)S(1)} fusion(bf16[8,4,256,512]{3,2,1,0:T(8,128)(2,1)} %get-tuple-element.15, bf16[4,256,512]{2,1,0:T(8,128)(2,1)} %h_ref.1), kind=kOutput, calls=%fused_computation.13 | convolution fusion | flops 2147483648 | bytes 11534336 | tf_op jit(solution)/shard_map/dot_general | solution.py:331
  146.8 0.0 copy-done.8
  146.8 0.0 copy-done.14
  146.8 0.0 copy-start.12
  146.8 2.4 fusion.2
  149.2 0.0 copy-start
  149.3 0.0 copy-done.12
  149.3 0.0 copy-start.11
  149.3 2.6 fusion.14.px_ref
  151.9 0.0 copy-done
  151.9 0.5 copy-done.11
  152.4 4.4 fusion.15.py_ref
  156.8 41.3 %exchange.3 = (f32[2048,256]{1,0:T(8,128)}, f32[2048,256]{1,0:T(8,128)}) custom-call(f32[256,256]{1,0:T(8,128)} %fusion.14.px_ref, f32[512,256]{1,0:T(8,128)} %fusion.15.py_ref), custom_call_target="tpu_custom_call" | custom-call | tf_op jit(solution)/shard_map/exchange/pallas_call | solution.py:204
  198.2 0.0 copy-start.4
  198.2 6.2 %convolution_bitcast_fusion.6 = f32[1,256,256]{2,1,0:T(8,128)S(1)} fusion(f32[2048,256]{1,0:T(8,128)} %get-tuple-element.19), kind=kOutput, calls=%fused_computation.8 | convolution fusion | flops 1610612736 | bytes 2359296 | tf_op jit(solution)/shard_map/dot_general | solution.py:320
  204.4 0.0 copy-done.4
  204.4 3.6 convolution_bitcast_fusion.5
  208.0 0.9 pad_maximum_fusion.inner_ref
  208.9 27.7 %inverse_factors.3 = f32[2,256,256]{2,1,0:T(8,128)} custom-call(f32[2,256,256]{2,1,0:T(8,128)} %pad_maximum_fusion.inner_ref), custom_call_target="tpu_custom_call" | custom-call | tf_op jit(solution)/shard_map/inverse_factors/pallas_call | solution.py:72
  236.6 2.8 fusion.9
  239.4 0.0 copy-done.2
  239.4 0.0 copy-done.9
  239.4 0.0 copy-start.1
  239.4 1.0 fusion.10
  240.4 1.1 copy-done.1
  241.6 4.4 fusion.17.py_ref
  246.0 2.6 fusion.16.px_ref
  248.6 41.1 %exchange.4 = (f32[2048,256]{1,0:T(8,128)}, f32[2048,256]{1,0:T(8,128)}) custom-call(f32[256,256]{1,0:T(8,128)} %fusion.16.px_ref, f32[512,256]{1,0:T(8,128)} %fusion.17.py_ref), custom_call_target="tpu_custom_call" | custom-call | tf_op jit(solution)/shard_map/exchange/pallas_call | solution.py:204
  289.8 0.0 copy-start.5
  289.8 6.0 %convolution_bitcast_fusion.4 = f32[1,256,256]{2,1,0:T(8,128)S(1)} fusion(f32[2048,256]{1,0:T(8,128)} %get-tuple-element.21), kind=kOutput, calls=%fused_computation.6 | convolution fusion | flops 1610612736 | bytes 2359296 | tf_op jit(solution)/shard_map/dot_general | solution.py:320
  295.8 0.0 copy-done.5
  295.8 3.6 convolution_bitcast_fusion.3
  299.5 0.9 pad_maximum_fusion.1.inner_ref
  300.4 27.9 %inverse_factors.4 = f32[2,256,256]{2,1,0:T(8,128)} custom-call(f32[2,256,256]{2,1,0:T(8,128)} %pad_maximum_fusion.1.inner_ref), custom_call_target="tpu_custom_call" | custom-call | tf_op jit(solution)/shard_map/inverse_factors/pallas_call | solution.py:72
  328.2 4.2 fusion.7
  332.4 0.0 copy-done.3
  332.4 2.4 fusion.8
  334.8 7.2 %fusion.19.py_ref = f32[512,256]{1,0:T(8,128)} fusion(f32[512,2048]{0,1:T(8,128)} %bitcast.90, f32[2048,256]{1,0:T(8,128)} %fusion.7), kind=kOutput, calls=%fused_computation.39 | convolution fusion | flops 1610612736 | bytes 6815744 | tf_op jit(solution)/shard_map/dot_general | solution.py:320
  342.0 2.6 fusion.18.px_ref
  344.6 41.9 %exchange.5 = (f32[2048,256]{1,0:T(8,128)}, f32[2048,256]{1,0:T(8,128)}) custom-call(f32[256,256]{1,0:T(8,128)} %fusion.18.px_ref, f32[512,256]{1,0:T(8,128)} %fusion.19.py_ref), custom_call_target="tpu_custom_call" | custom-call | tf_op jit(solution)/shard_map/exchange/pallas_call | solution.py:204
  386.6 0.0 copy-start.6
  386.6 6.0 %convolution_bitcast_fusion.2 = f32[1,256,256]{2,1,0:T(8,128)S(1)} fusion(f32[2048,256]{1,0:T(8,128)} %get-tuple-element.23), kind=kOutput, calls=%fused_computation.4 | convolution fusion | flops 1610612736 | bytes 2359296 | tf_op jit(solution)/shard_map/dot_general | solution.py:320
  392.6 3.5 convolution_bitcast_fusion.1
  396.1 0.8 pad_maximum_fusion.2.inner_ref
  397.0 27.7 %inverse_factors.5 = f32[2,256,256]{2,1,0:T(8,128)} custom-call(f32[2,256,256]{2,1,0:T(8,128)} %pad_maximum_fusion.2.inner_ref), custom_call_target="tpu_custom_call" | custom-call | tf_op jit(solution)/shard_map/inverse_factors/pallas_call | solution.py:72
  424.6 1.4 fusion.1
  426.0 1.8 convolution_bitcast_fusion
  427.8 0.0 reduce-scatter.5.cloned.1.call-update
  427.8 0.0 reduce-scatter.7.cloned.1.call-start
  427.9 1.0 copy-done.13
  428.8 0.4 fusion
  429.3 40.3 %reduce-scatter.5.cloned.1.call-done = f32[4,32,512]{2,1,0:T(8,128)} async-done(((f32[4,256,512]{2,1,0:T(8,128)}), f32[4,32,512]{2,1,0:T(8,128)}) %reduce-scatter.5.cloned.1.call-update) | async-done | bytes 262160 | tf_op jit(solution)/shard_map/reduce_scatter | solution.py:349
  469.6 1.2 fusion.20
  470.8 0.2 copy.9
  471.0 0.9 reshape.13
  472.0 0.0 reduce-scatter.7.cloned.1.call-update
  472.0 19.6 %reduce-scatter.7.cloned.1.call-done = f32[64,128]{1,0:T(8,128)} async-done(((f32[256,128]{1,0:T(8,128)}), f32[64,128]{1,0:T(8,128)}) %reduce-scatter.7.cloned.1.call-update) | async-done | bytes 32784
  491.6 0.9 reshape.14
  492.5 0.7 copy.10
  (9 shorter events, 0.0 us)
Async XLA Ops:
  6.5 463.1 %reduce-scatter.5.cloned.1.call-start = ((), (), s32[]{:S(2)}) async-start(), calls=%async_computation.2 | async-start | bytes 2359296 | tf_op jit(solution)/shard_map/reduce_scatter | solution.py:349
  140.6 6.2 %copy-start.8 = (bf16[4,256,512]{2,1,0:T(8,128)(2,1)S(1)}, bf16[4,256,512]{2,1,0:T(8,128)(2,1)}, u32[]{:S(2)}) copy-start(bf16[4,256,512]{2,1,0:T(8,128)(2,1)} %h_ref.1) | copy-start | bytes 3145732
  140.7 6.2 %copy-start.14 = (bf16[4,4,256,512]{3,2,1,0:T(8,128)(2,1)S(1)}, bf16[4,4,256,512]{3,2,1,0:T(8,128)(2,1)}, u32[]{:S(2)}) copy-start(bf16[4,4,256,512]{3,2,1,0:T(8,128)(2,1)} %get-tuple-element.17) | copy-start | bytes 12582916
  146.8 2.4 copy-start.12
  149.2 2.6 copy-start
  149.3 3.2 copy-start.11
  198.2 6.2 %copy-start.4 = (f32[2048,256]{1,0:T(8,128)S(1)}, f32[2048,256]{1,0:T(8,128)}, u32[]{:S(2)}) copy-start(f32[2048,256]{1,0:T(8,128)} %get-tuple-element.20) | copy-start | bytes 6291460
  236.6 2.8 copy-start.2
  236.6 2.8 copy-start.9
  239.4 2.2 copy-start.1
  289.8 6.1 %copy-start.5 = (f32[2048,256]{1,0:T(8,128)S(1)}, f32[2048,256]{1,0:T(8,128)}, u32[]{:S(2)}) copy-start(f32[2048,256]{1,0:T(8,128)} %get-tuple-element.22) | copy-start | bytes 6291460
  328.2 4.2 copy-start.3
  328.2 4.2 copy-start.10
  334.8 7.2 %copy-start.7 = (f32[2048,256]{1,0:T(8,128)S(1)}, f32[2048,256]{1,0:T(8,128)}, u32[]{:S(2)}) copy-start(f32[2048,256]{1,0:T(8,128)} %fusion.8) | copy-start | bytes 6291460
  386.6 6.0 %copy-start.6 = (f32[2048,256]{1,0:T(8,128)S(1)}, f32[2048,256]{1,0:T(8,128)}, u32[]{:S(2)}) copy-start(f32[2048,256]{1,0:T(8,128)} %get-tuple-element.24) | copy-start | bytes 6291460
  427.8 1.0 copy-start.13
  427.8 63.8 %reduce-scatter.7.cloned.1.call-start = ((), (), s32[]{:S(2)}) async-start(), calls=%async_computation.3 | async-start | bytes 163840
Sparse Core Ops, SparseCore 0:
  427.9 41.5 reduce-scatter.4
  472.1 19.4 reduce-scatter.6
